TPU v7x, 128 devices: a whole 4x4x4 slice. The times are simulated.
128 devices in a mesh: row: 32 (over x_hi, z, y), ch: 4 (over x_lo, core).
Axes of the slice: x: 4 (x_hi: 2, x_lo: 2; x = x_hi * 2 + x_lo), y: 4, z: 4, core: 2. Of those that a mesh axis runs over, the one named last changes fastest.
Arguments:
- pair_rep: float32 [256, 256, 128], P(('row', 'ch')), may hold values from -6 to 6
- pair_mask: int32 [256, 256], P(('row', 'ch')), may hold values from 0 to 1, as said below
- ln_in_gain: float32 [128], replicated, may hold values from 0.5 to 1.5
- ln_in_bias: float32 [128], replicated, may hold values from -3 to 3
- w_in: float32 [128, 640], replicated, may hold values from -0.5 to 0.5
- b_in: float32 [640], replicated, may hold values from -3 to 3
- ln_out_gain: float32 [128], replicated, may hold values from 0.5 to 1.5
- ln_out_bias: float32 [128], replicated, may hold values from -3 to 3
- w_out: float32 [128, 128], replicated, may hold values from -0.5 to 0.5
- b_out: float32 [128], replicated, may hold values from -3 to 3
- cotangent: float32 [256, 256, 128], P(('row', 'ch')), may hold values from -6 to 6
Outputs:
- update: float32 [256, 256, 128], P(('row', 'ch'))
- grad_pair: float32 [256, 256, 128], P(('row', 'ch'))
- grad_w_in: float32 [128, 640], replicated
- grad_w_out: float32 [128, 128], replicated
Inputs may be any that keep to these rules, and one draw needn't show every extreme that they name: pair_mask[i, k] = m_i m_k, where m is 1 for the residues present in the crop and 0 otherwise.
All inputs are finite; a program needn't handle non-finite values.
Results may differ from a plain program's by a relative error of at most 0.00009.
Values sent between devices are 32-bit elements; how exact they have to be, the bound alone decides.
No kernel may reach another device: no remote copies, remote signals or barrier semaphores. Data moves between devices by JAX's collectives and lax.ppermute only.
A program may use at most 64 MiB of HBM per device.

v0:
```python
import jax
import jax.numpy as jnp
from jax import lax
from jax.sharding import PartitionSpec as P

epsilon = 1e-05


def side_by_side(arrays, axis, split_dim, concat_dim, along):
    ends, at = ([], 0)
    for a in arrays[:-1]:
        at += a.shape[along]
        ends.append(at)
    both = jnp.concatenate(arrays, axis=along)
    return tuple(
        jnp.split(
            lax.all_to_all(both, axis, split_axis=split_dim, concat_axis=concat_dim, tiled=True),
            ends,
            axis=along,
        )
    )


def prelude(field, keep_mask, norm_gain, norm_bias, weights, offsets):
    channels = field.shape[-1]
    hidden = (weights.shape[1] - channels) // 4
    center = jnp.mean(field, -1, keepdims=True)
    spread = jnp.mean((field - center) ** 2, -1, keepdims=True)
    normed = (field - center) * lax.rsqrt(spread + epsilon) * norm_gain + norm_bias
    pieces = jnp.einsum(
        "ikc,cf->fik", normed, weights[:, : 4 * hidden], precision=lax.Precision.HIGHEST
    )
    pieces = pieces + offsets[: 4 * hidden, None, None]
    gate = jax.nn.sigmoid(
        jnp.einsum("ikc,cf->ikf", normed, weights[:, 4 * hidden :], precision=lax.Precision.HIGHEST)
        + offsets[4 * hidden :]
    )
    keep = keep_mask.astype(field.dtype)[None]
    left = keep * jax.nn.sigmoid(pieces[:hidden]) * pieces[hidden : 2 * hidden]
    right = keep * jax.nn.sigmoid(pieces[2 * hidden : 3 * hidden]) * pieces[3 * hidden :]
    return (left, right, gate)


def epilogue(product, gate, norm_gain, norm_bias, weights, offset):
    center = jnp.mean(product, 0, keepdims=True)
    spread = jnp.mean((product - center) ** 2, 0, keepdims=True)
    normed = (product - center) * lax.rsqrt(spread + epsilon) * norm_gain[
        :, None, None
    ] + norm_bias[:, None, None]
    projected = jnp.einsum("hij,hc->ijc", normed, weights, precision=lax.Precision.HIGHEST) + offset
    return gate * projected


def on_device(
    pair_rep,
    pair_mask,
    ln_in_gain,
    ln_in_bias,
    w_in,
    b_in,
    ln_out_gain,
    ln_out_bias,
    w_out,
    b_out,
    cotangent,
):
    row_count = pair_rep.shape[0]
    length = pair_rep.shape[1]
    hidden = w_out.shape[0]
    per_device = hidden // (lax.axis_size("row") * lax.axis_size("ch"))

    def local_prelude(field, weights):
        return prelude(field, pair_mask, ln_in_gain, ln_in_bias, weights, b_in)

    (left_rows, right_rows, gate), prelude_back = jax.vjp(local_prelude, pair_rep, w_in)
    row_shape = (hidden, 1, row_count, length)
    left_cols, right_cols = side_by_side(
        (left_rows.reshape(row_shape), right_rows.reshape(row_shape)), ("row", "ch"), 0, 2, 1
    )
    left_cols = left_cols.reshape(per_device, length, length)
    right_cols = right_cols.reshape(per_device, length, length)
    product = jnp.einsum("hik,hjk->hij", left_cols, right_cols, precision=lax.Precision.HIGHEST)
    product_rows = lax.all_to_all(
        product.reshape(per_device, 1, length, length),
        ("row", "ch"),
        split_axis=2,
        concat_axis=0,
        tiled=True,
    )
    product_rows = product_rows.reshape(hidden, row_count, length)

    def local_epilogue(prod_part, gate_part, weights):
        return epilogue(prod_part, gate_part, ln_out_gain, ln_out_bias, weights, b_out)

    update, epilogue_back = jax.vjp(local_epilogue, product_rows, gate, w_out)
    d_product, d_gate, d_wout = epilogue_back(cotangent)
    d_cols = lax.all_to_all(
        d_product.reshape(row_shape), ("row", "ch"), split_axis=0, concat_axis=2, tiled=True
    )
    d_cols = d_cols.reshape(per_device, length, length)
    d_left = jnp.einsum("hij,hjk->hik", d_cols, right_cols, precision=lax.Precision.HIGHEST)
    d_right = jnp.einsum("hij,hik->hjk", d_cols, left_cols, precision=lax.Precision.HIGHEST)
    col_shape = (per_device, 1, length, length)
    d_left, d_right = side_by_side(
        (d_left.reshape(col_shape), d_right.reshape(col_shape)), ("row", "ch"), 2, 0, 1
    )
    d_left = d_left.reshape(hidden, row_count, length)
    d_right = d_right.reshape(hidden, row_count, length)
    grad_pair, d_win = prelude_back((d_left, d_right, d_gate))
    d_win, d_wout = lax.psum((d_win, d_wout), ("row", "ch"))
    return (update, grad_pair, d_win / length, d_wout / length)


def solution(mesh):
    placed = (
        P(("row", "ch"), None, None),
        P(("row", "ch"), None),
        P(),
        P(),
        P(),
        P(),
        P(),
        P(),
        P(),
        P(),
        P(("row", "ch"), None, None),
    )
    return jax.shard_map(
        on_device,
        mesh=mesh,
        in_specs=placed,
        out_specs=(P(("row", "ch"), None, None), P(("row", "ch"), None, None), P(), P()),
        check_vma=False,
    )
```

profile of v0, /device:TPU:1, one launch (start us, length us, event | category | flops | bytes accessed | tf_op | source)
XLA Modules:
  0.0 247.7 jit_solution(5997997700631045639)
XLA Ops:
  7.2 0.7 convert_element_type.3
  7.9 1.1 copy.48
  9.3 0.7 copy-done.3
  10.0 1.1 fusion
  11.6 24.7 %all_to_all.54 = f32[128,2,2,256]{3,2,1,0:T(2,128)S(1)} all-to-all(f32[128,2,2,256]{3,2,1,0:T(2,128)S(1)} %copy.51), channel_id=1, replica_groups=mesh['row'=32,'ch'=4] {'row','ch'}, dimensions={0} | all-to-all | bytes 1048576 | tf_op jit(solution)/shard_map/all_to_all | solution.py:17
  36.7 0.4 fusion.51
  37.1 0.4 convolution_bitcast_fusion.2
  37.5 1.0 copy.53
  38.5 4.9 %all-to-all-start.1 = ((f32[1,1,256,256]{3,1,0,2:T(1,128)}), f32[1,1,256,256]{3,1,0,2:T(1,128)S(1)}, u32[]{:S(2)}, u32[]{:S(2)}) async-start(f32[1,1,256,256]{3,1,0,2:T(1,128)} %copy.53), calls=%async_computation.1 | async-start | bytes 524288 | tf_op jit(solution)/shard_map/all_to_all | solution.py:83
  43.4 0.7 fusion.6
  44.1 10.3 %all-to-all-done.1 = f32[1,1,256,256]{3,1,0,2:T(1,128)S(1)} async-done(((f32[1,1,256,256]{3,1,0,2:T(1,128)}), f32[1,1,256,256]{3,1,0,2:T(1,128)S(1)}, u32[]{:S(2)}, u32[]{:S(2)}) %all-to-all-start.1) | async-done | bytes 262176 | tf_op jit(solution)/shard_map/all_to_all | solution.py:83
  54.3 0.6 reduce
  55.3 0.8 copy-done.1
  56.1 0.4 multiply_reduce_fusion.1
  56.9 15.3 %all_to_all.55 = f32[128,1,2,256]{3,2,1,0:T(2,128)S(1)} all-to-all(f32[128,1,2,256]{3,2,1,0:T(2,128)S(1)} %copy.56), channel_id=1, replica_groups=mesh['row'=32,'ch'=4] {'row','ch'}, dimensions={0} | all-to-all | bytes 524288 | tf_op jit(solution)/shard_map/all_to_all | solution.py:97
  72.4 0.6 convolution_bitcast_fusion
  73.0 0.4 convolution_bitcast_fusion.1
  73.4 1.2 copy.57
  74.6 4.5 %all-to-all-start.3 = ((f32[1,2,256,256]{3,1,0,2:T(2,128)}), f32[1,2,256,256]{3,1,0,2:T(2,128)S(1)}, u32[]{:S(2)}, u32[]{:S(2)}) async-start(f32[1,2,256,256]{3,1,0,2:T(2,128)} %copy.57), calls=%async_computation.3 | async-start | bytes 1048576 | tf_op jit(solution)/shard_map/all_to_all | solution.py:17
  79.4 1.1 convolution_bitcast_fusion.4
  80.4 1.4 fusion.52
  81.8 0.5 convolution_bitcast_fusion.5
  82.3 10.3 %all-to-all-done.3 = f32[1,2,256,256]{3,1,0,2:T(2,128)S(1)} async-done(((f32[1,2,256,256]{3,1,0,2:T(2,128)}), f32[1,2,256,256]{3,1,0,2:T(2,128)S(1)}, u32[]{:S(2)}, u32[]{:S(2)}) %all-to-all-start.3) | async-done | bytes 524320 | tf_op jit(solution)/shard_map/all_to_all | solution.py:17
  93.1 0.6 copy-done.8
  93.7 0.8 convolution_bitcast_fusion.3
  94.7 1.2 fusion.7
  95.9 0.5 multiply_reduce_fusion.5
  96.5 0.7 pad_add_fusion.3
  97.3 0.8 copy.61
  98.2 140.3 %all-reduce.9.cloned.1.call-done = (f32[128,640]{1,0:T(8,128)}, f32[128,128]{1,0:T(8,128)}) async-done(((f32[128,640]{1,0:T(8,128)}, f32[128,128]{1,0:T(8,128)}), (f32[128,640]{1,0:T(8,128)}, f32[128,128]{1,0:T(8,128)})) %all-reduce.9.cloned.1.call-update) | async-done | bytes 393232 | tf_op jit(solution)/shard_map/psum | solution.py:110
  238.4 1.8 broadcast_multiply_fusion
  240.2 0.6 broadcast_multiply_fusion.1
  (54 shorter events, 2.9 us)
Async XLA Ops:
  7.2 48.1 %copy-start = (f32[128,128]{1,0:T(8,128)S(1)}, f32[128,128]{1,0:T(8,128)}, u32[]{:S(2)}) copy-start(f32[128,128]{1,0:T(8,128)} %param.19) | copy-start | bytes 196612
  7.9 1.2 copy-start.2
  9.1 1.0 copy-start.3
  9.3 0.8 slice-start
  9.3 0.7 copy-start.7
  9.3 0.7 copy-start.10
  38.5 4.9 %copy-start.6 = (f32[640]{0:T(1024)S(1)}, f32[640]{0:T(1024)}, u32[]{:S(2)}) copy-start(f32[640]{0:T(1024)} %param.16) | copy-start | bytes 7684
  38.5 15.9 %all-to-all-start.1 = ((f32[1,1,256,256]{3,1,0,2:T(1,128)}), f32[1,1,256,256]{3,1,0,2:T(1,128)S(1)}, u32[]{:S(2)}, u32[]{:S(2)}) async-start(f32[1,1,256,256]{3,1,0,2:T(1,128)} %copy.53), calls=%async_computation.1 | async-start | bytes 524288 | tf_op jit(solution)/shard_map/all_to_all | solution.py:83
  55.1 1.0 copy-start.1
  55.3 0.8 copy-start.9
  74.6 4.8 %copy-start.12 = (f32[128]{0:T(128)S(1)}, f32[128]{0:T(128)}, u32[]{:S(2)}) copy-start(f32[128]{0:T(128)} %param.18) | copy-start | bytes 1540
  74.6 18.0 %all-to-all-start.3 = ((f32[1,2,256,256]{3,1,0,2:T(2,128)}), f32[1,2,256,256]{3,1,0,2:T(2,128)S(1)}, u32[]{:S(2)}, u32[]{:S(2)}) async-start(f32[1,2,256,256]{3,1,0,2:T(2,128)} %copy.57), calls=%async_computation.3 | async-start | bytes 1048576 | tf_op jit(solution)/shard_map/all_to_all | solution.py:17
  79.1 1.3 copy-start.13
  79.1 159.3 %all-reduce.9.cloned.1.call-start = ((), (), s32[]{:S(2)}) async-start(), calls=%async_computation.4 | async-start | bytes 786432 | tf_op jit(solution)/shard_map/psum | solution.py:110
  93.1 0.7 copy-start.8
  93.1 0.7 copy-start.11
  93.7 1.0 copy-start.4
  238.4 1.8 copy-start.5
Sparse Core Ops, SparseCore 0:
  97.4 141.0 all-reduce.8
where the time goes:
time: 248 us
  waiting for transfers between devices  161 us (65%)
  blocking collectives  40 us (16%)
  between operations  14.4 us (6%)
  starting transfers between devices  9.62 us (4%)
  matrix products  8.93 us (4%)
  local copies, waits for them, and re-layouts  8.28 us (3%)
  other arithmetic  5.56 us (2%)
    psum x1, waiting for transfers between devices, on_device(): d_win, d_wout = lax.psum((d_win, d_wout), ('row', 'ch'))  140 us
    all_to_all x1, blocking collectives, side_by_side(): lax.all_to_all(both, axis, split_axis=split_dim, concat_axis=concat_dim,...  24.7 us
    all_to_all x1, blocking collectives, on_device(): lax.all_to_all(d_product.reshape(row_shape), ('row', 'ch'), split_axis=0,...  15.3 us
    all_to_all x1, waiting for transfers between devices, side_by_side(): lax.all_to_all(both, axis, split_axis=split_dim, concat_axis=concat_dim,...  10.3 us
    all_to_all x1, waiting for transfers between devices, on_device(): lax.all_to_all(product.reshape(per_device, 1, length, length), ('row', 'c...  10.3 us
  transfers between devices with their start and end apart: 3, of which 3 were waited for; matrix products, arithmetic and copies ran while one was open for 2% of the time, Pallas kernels for 0%

commit v1 on v0

--- a/solution.py
+++ b/solution.py
@@ -107,7 +107,7 @@
     d_left = d_left.reshape(hidden, row_count, length)
     d_right = d_right.reshape(hidden, row_count, length)
     grad_pair, d_win = prelude_back((d_left, d_right, d_gate))
-    d_win, d_wout = lax.psum((d_win, d_wout), ("row", "ch"))
+    d_win, d_wout = lax.psum(lax.psum((d_win, d_wout), "row"), "ch")
     return (update, grad_pair, d_win / length, d_wout / length)
 
 

time: 248 us -> 480 us (1.94)
  waiting for transfers between devices: 161 us -> 393 us
    psum x1 -> x2, waiting for transfers between devices: 140 us -> 372 us  [on_device(): d_win, d_wout = lax.psum(lax.psum((d_win, d_wout), 'row'), 'ch')]
  transfers between devices with their start and end apart: 3 -> 4, of which waited for: 3 -> 4; matrix products, arithmetic and copies ran while one was open for 2% -> 1% of each run, Pallas kernels for 0% -> 0%
where the time goes in v1:
time: 480 us
  waiting for transfers between devices  393 us (82%)
  blocking collectives  40 us (8%)
  between operations  14.4 us (3%)
  starting transfers between devices  9.67 us (2%)
  matrix products  8.92 us (2%)
  local copies, waits for them, and re-layouts  8.28 us (2%)
  other arithmetic  5.56 us (1%)
    psum x2, waiting for transfers between devices, on_device(): d_win, d_wout = lax.psum(lax.psum((d_win, d_wout), 'row'), 'ch')  372 us
    all_to_all x1, blocking collectives, side_by_side(): lax.all_to_all(both, axis, split_axis=split_dim, concat_axis=concat_dim,...  24.7 us
    all_to_all x1, blocking collectives, on_device(): lax.all_to_all(d_product.reshape(row_shape), ('row', 'ch'), split_axis=0,...  15.3 us
    all_to_all x1, waiting for transfers between devices, side_by_side(): lax.all_to_all(both, axis, split_axis=split_dim, concat_axis=concat_dim,...  10.3 us
    all_to_all x1, waiting for transfers between devices, on_device(): lax.all_to_all(product.reshape(per_device, 1, length, length), ('row', 'c...  10.3 us
  transfers between devices with their start and end apart: 4, of which 4 were waited for; matrix products, arithmetic and copies ran while one was open for 1% of the time, Pallas kernels for 0%

profile of v1, /device:TPU:1, one launch (start us, length us, event | category | flops | bytes accessed | tf_op | source)
XLA Modules:
  0.0 479.7 jit_solution(8070673602340824726)
XLA Ops:
  7.2 0.7 convert_element_type.3
  7.9 1.1 copy.48
  9.3 0.7 copy-done.3
  10.0 1.1 fusion
  11.6 24.7 %all_to_all.54 = f32[128,2,2,256]{3,2,1,0:T(2,128)S(1)} all-to-all(f32[128,2,2,256]{3,2,1,0:T(2,128)S(1)} %copy.51), channel_id=1, replica_groups=mesh['row'=32,'ch'=4] {'row','ch'}, dimensions={0} | all-to-all | bytes 1048576 | tf_op jit(solution)/shard_map/all_to_all | solution.py:17
  36.7 0.4 fusion.51
  37.1 0.4 convolution_bitcast_fusion.2
  37.5 1.0 copy.53
  38.5 4.9 %all-to-all-start.1 = ((f32[1,1,256,256]{3,1,0,2:T(1,128)}), f32[1,1,256,256]{3,1,0,2:T(1,128)S(1)}, u32[]{:S(2)}, u32[]{:S(2)}) async-start(f32[1,1,256,256]{3,1,0,2:T(1,128)} %copy.53), calls=%async_computation.1 | async-start | bytes 524288 | tf_op jit(solution)/shard_map/all_to_all | solution.py:83
  43.4 0.7 fusion.6
  44.1 10.3 %all-to-all-done.1 = f32[1,1,256,256]{3,1,0,2:T(1,128)S(1)} async-done(((f32[1,1,256,256]{3,1,0,2:T(1,128)}), f32[1,1,256,256]{3,1,0,2:T(1,128)S(1)}, u32[]{:S(2)}, u32[]{:S(2)}) %all-to-all-start.1) | async-done | bytes 262176 | tf_op jit(solution)/shard_map/all_to_all | solution.py:83
  54.3 0.6 reduce
  55.3 0.8 copy-done.1
  56.1 0.4 multiply_reduce_fusion.1
  56.9 15.3 %all_to_all.55 = f32[128,1,2,256]{3,2,1,0:T(2,128)S(1)} all-to-all(f32[128,1,2,256]{3,2,1,0:T(2,128)S(1)} %copy.56), channel_id=1, replica_groups=mesh['row'=32,'ch'=4] {'row','ch'}, dimensions={0} | all-to-all | bytes 524288 | tf_op jit(solution)/shard_map/all_to_all | solution.py:97
  72.4 0.6 convolution_bitcast_fusion
  73.4 1.2 copy.57
  74.6 4.5 all-to-all-start.3
  79.4 1.1 convolution_bitcast_fusion.4
  80.4 1.4 fusion.52
  81.8 0.5 convolution_bitcast_fusion.5
  82.3 10.3 %all-to-all-done.3 = f32[1,2,256,256]{3,1,0,2:T(2,128)S(1)} async-done(((f32[1,2,256,256]{3,1,0,2:T(2,128)}), f32[1,2,256,256]{3,1,0,2:T(2,128)S(1)}, u32[]{:S(2)}, u32[]{:S(2)}) %all-to-all-start.3) | async-done | bytes 524320 | tf_op jit(solution)/shard_map/all_to_all | solution.py:17
  93.1 0.6 copy-done.8
  93.7 0.8 convolution_bitcast_fusion.3
  94.7 1.2 fusion.7
  95.9 0.7 pad_add_fusion.3
  96.7 0.5 multiply_reduce_fusion.5
  97.3 315.4 %all-reduce.11.cloned.1.call-done = (f32[128,640]{1,0:T(8,128)}, f32[128,128]{1,0:T(8,128)}) async-done(((f32[128,640]{1,0:T(8,128)}, f32[128,128]{1,0:T(8,128)}), (f32[128,640]{1,0:T(8,128)}, f32[128,128]{1,0:T(8,128)})) %all-reduce.11.cloned.1.call-update) | async-done | bytes 393232 | tf_op jit(solution)/shard_map/psum | solution.py:110
  412.8 0.8 copy.61
  413.6 56.9 %all-reduce.13.cloned.1.call-done = (f32[128,640]{1,0:T(8,128)}, f32[128,128]{1,0:T(8,128)}) async-done(((f32[128,640]{1,0:T(8,128)}, f32[128,128]{1,0:T(8,128)}), (f32[128,640]{1,0:T(8,128)}, f32[128,128]{1,0:T(8,128)})) %all-reduce.13.cloned.1.call-update) | async-done | bytes 393232 | tf_op jit(solution)/shard_map/psum | solution.py:110
  470.5 1.8 broadcast_multiply_fusion
  472.3 0.6 broadcast_multiply_fusion.1
  (57 shorter events, 3.4 us)
Async XLA Ops:
  7.2 48.1 %copy-start = (f32[128,128]{1,0:T(8,128)S(1)}, f32[128,128]{1,0:T(8,128)}, u32[]{:S(2)}) copy-start(f32[128,128]{1,0:T(8,128)} %param.19) | copy-start | bytes 196612
  7.9 1.2 copy-start.2
  9.1 1.0 copy-start.3
  9.3 0.8 slice-start
  9.3 0.7 copy-start.7
  9.3 0.7 copy-start.10
  38.5 4.9 %copy-start.6 = (f32[640]{0:T(1024)S(1)}, f32[640]{0:T(1024)}, u32[]{:S(2)}) copy-start(f32[640]{0:T(1024)} %param.16) | copy-start | bytes 7684
  38.5 15.9 %all-to-all-start.1 = ((f32[1,1,256,256]{3,1,0,2:T(1,128)}), f32[1,1,256,256]{3,1,0,2:T(1,128)S(1)}, u32[]{:S(2)}, u32[]{:S(2)}) async-start(f32[1,1,256,256]{3,1,0,2:T(1,128)} %copy.53), calls=%async_computation.1 | async-start | bytes 524288 | tf_op jit(solution)/shard_map/all_to_all | solution.py:83
  55.1 1.0 copy-start.1
  55.3 0.8 copy-start.9
  74.6 4.8 copy-start.12
  74.6 18.0 %all-to-all-start.3 = ((f32[1,2,256,256]{3,1,0,2:T(2,128)}), f32[1,2,256,256]{3,1,0,2:T(2,128)S(1)}, u32[]{:S(2)}, u32[]{:S(2)}) async-start(f32[1,2,256,256]{3,1,0,2:T(2,128)} %copy.57), calls=%async_computation.3 | async-start | bytes 1048576 | tf_op jit(solution)/shard_map/all_to_all | solution.py:17
  79.1 1.3 copy-start.13
  79.1 333.6 %all-reduce.11.cloned.1.call-start = ((), (), s32[]{:S(2)}) async-start(), calls=%async_computation.4 | async-start | bytes 786432 | tf_op jit(solution)/shard_map/psum | solution.py:110
  93.1 0.7 copy-start.8
  93.1 0.7 copy-start.11
  93.7 1.0 copy-start.4
  96.7 373.8 %all-reduce.13.cloned.1.call-start = ((), (), s32[]{:S(2)}) async-start(), calls=%async_computation.5 | async-start | bytes 786432 | tf_op jit(solution)/shard_map/psum | solution.py:110
  470.5 1.8 copy-start.5
Sparse Core Ops, SparseCore 0:
  96.8 315.8 all-reduce.10
  415.4 55.0 all-reduce.12
